TPU v7x, 128 devices: a whole 4x4x4 slice. The times are simulated.
128 devices in a mesh: dp: 16 (over y_hi, x, core), hid: 8 (over y_lo, z).
Axes of the slice: x: 4, y: 4 (y_hi: 2, y_lo: 2; y = y_hi * 2 + y_lo), z: 4, core: 2. Of those that a mesh axis runs over, the one named last changes fastest.
Arguments:
- train_x: bfloat16 [4096, 4096], P('dp', 'hid'), may hold values from -6 to 6
- gate_pre: bfloat16 [4096, 14336], P('dp', 'hid'), may hold values from -6 to 6
- up_pre: bfloat16 [4096, 14336], P('dp', 'hid'), may hold values from -6 to 6
- train_dy: bfloat16 [4096, 4096], P('dp'), may hold values from -6 to 6
- val_x: bfloat16 [512, 4096], P('dp', 'hid'), may hold values from -6 to 6
- val_gate: bfloat16 [512, 14336], P('dp', 'hid'), may hold values from -6 to 6
- val_up: bfloat16 [512, 14336], P('dp', 'hid'), may hold values from -6 to 6
- val_dy: bfloat16 [512, 4096], P('dp'), may hold values from -6 to 6
- down_weight: bfloat16 [14336, 4096], P('hid', 'dp'), may hold values from -0.046875 to 0.046875
Outputs:
- gate_grad: bfloat16 [4096, 14336], P('dp', 'hid')
- up_grad: bfloat16 [4096, 14336], P('dp', 'hid')
- scores: float32 [16, 2], P('dp')
All inputs are finite; a program needn't handle non-finite values.
Results may differ from a plain program's by a relative error of at most 0.0059.
Values may be sent and summed in bfloat16 or wider, within the bound.
A program may use at most 128 MiB of HBM per device.

v0:
```python
import jax
import jax.numpy as jnp
from jax import lax
from jax.sharding import PartitionSpec as P

LEN = 256
step_rate = 0.1


def side_by_side(arrays, axis, dim, along):
    widths = [a.shape[along] for a in arrays]
    both = jnp.concatenate(arrays, axis=along)
    filled = lax.all_gather(both, axis, axis=dim, tiled=True)
    return tuple(jnp.split(filled, [sum(widths[:k]) for k in range(1, len(widths))], axis=along))


def cut_along(shard, dim, peers):
    before, after = (shard.shape[:dim], shard.shape[dim + 1 :])
    return jnp.moveaxis(shard.reshape(*before, peers, -1, *after), dim, 0)


def sum_at_owner(shard, axis, dim):
    parts = cut_along(shard, dim, lax.axis_size(axis))
    arrived = lax.all_to_all(parts, axis, split_axis=0, concat_axis=0, tiled=True)
    return arrived.sum(axis=0)


def sent_to_all(shard, axis):
    copies = jnp.broadcast_to(shard, (lax.axis_size(axis), *shard.shape))
    return lax.all_to_all(copies, axis, split_axis=0, concat_axis=0, tiled=True)


def over_copies(shard, axis):
    return sent_to_all(shard, axis).sum(axis=0)


def backward_parts(hidden_cot, gate, up):
    a = gate.astype(jnp.float32)
    b = up.astype(jnp.float32)
    s = jax.nn.sigmoid(a)
    silu = a * s
    hidden = (silu * b).astype(jnp.bfloat16)
    gate_grad = (hidden_cot * b * s * (1.0 + a * (1.0 - s))).astype(jnp.bfloat16)
    up_grad = (hidden_cot * silu).astype(jnp.bfloat16)
    return (hidden, gate_grad, up_grad)


def pair_dot(left, right):
    return lax.dot_general(
        left, right, (((1,), (1,)), ((), ())), preferred_element_type=jnp.float32
    )


def per_device(train_x, gate_pre, up_pre, train_dy, val_x, val_gate, val_up, val_dy, down_weight):
    n_dp = lax.axis_size("dp")
    n_hid = lax.axis_size("hid")
    dp_me = lax.axis_index("dp")
    hid_me = lax.axis_index("hid")
    tok_rows = train_dy.shape[0]
    val_rows = val_dy.shape[0]
    width = train_x.shape[1]
    n_seq = tok_rows // LEN
    n_val = val_rows * n_dp // LEN
    piece = lax.all_gather(down_weight, "dp", axis=1, tiled=True)
    cot_train = pair_dot(train_dy, piece)
    cot_val = pair_dot(val_dy, piece)
    hidden, gate_grad, up_grad = backward_parts(cot_train, gate_pre, up_pre)
    val_hidden, val_gate_grad, val_up_grad = backward_parts(cot_val, val_gate, val_up)
    offset = hid_me * width
    train_feats = (
        train_x,
        jnp.concatenate([gate_grad, up_grad], axis=1),
        hidden,
        lax.dynamic_slice_in_dim(train_dy, offset, width, 1),
    )
    val_feats = (
        val_x,
        jnp.concatenate([val_gate_grad, val_up_grad], axis=1),
        val_hidden,
        lax.dynamic_slice_in_dim(val_dy, offset, width, 1),
    )
    share = tok_rows // n_hid
    row_seq = (hid_me * share + jnp.arange(share, dtype=jnp.int32)) // LEN
    seq_onehot = (row_seq[:, None] == jnp.arange(n_seq, dtype=jnp.int32)[None, :]).astype(
        jnp.float32
    )

    def grams(block):
        return jnp.stack([pair_dot(block[k], train_feats[k]) for k in range(4)])

    def absorb(state, block, source):
        return lax.dynamic_update_slice(state, grams(block), (0, source * val_rows, 0))

    state = jnp.zeros((4, n_dp * val_rows, tok_rows), jnp.float32)
    state = absorb(state, val_feats, dp_me)
    gathered = side_by_side((val_feats[0], val_feats[1], val_feats[2], val_feats[3]), "dp", 0, 1)

    def visit(step, current):
        source = (dp_me + step) % n_dp
        block = tuple(
            (lax.dynamic_slice_in_dim(whole, source * val_rows, val_rows, 0) for whole in gathered)
        )
        return absorb(current, block, source)

    state = lax.fori_loop(1, n_dp, visit, state)
    summed = sum_at_owner(state, "hid", 2)
    pair = summed[0] * summed[1] + summed[2] * summed[3]
    val_seq = jnp.arange(n_dp * val_rows, dtype=jnp.int32) // LEN
    val_onehot = (val_seq[:, None] == jnp.arange(n_val, dtype=jnp.int32)[None, :]).astype(
        jnp.float32
    )
    col_sums = jnp.dot(val_onehot.T, pair, precision=lax.Precision.HIGHEST)
    partial_scores = jnp.dot(col_sums, seq_onehot, precision=lax.Precision.HIGHEST).T
    scores = over_copies(partial_scores, "hid") * (-step_rate / (LEN * LEN))
    return (gate_grad, up_grad, scores)


def solution(mesh):
    return jax.shard_map(
        per_device,
        mesh=mesh,
        in_specs=(
            P("dp", "hid"),
            P("dp", "hid"),
            P("dp", "hid"),
            P("dp", None),
            P("dp", "hid"),
            P("dp", "hid"),
            P("dp", "hid"),
            P("dp", None),
            P("hid", "dp"),
        ),
        out_specs=(P("dp", "hid"), P("dp", "hid"), P("dp", None)),
        check_vma=False,
    )
```

profile of v0, /device:TPU:0, one launch (start us, length us, event | category | flops | bytes accessed | tf_op | source)
XLA Modules:
  0.0 357.7 jit_solution(11475155400102362533)
XLA Ops:
  8.7 115.3 %all-gather.3.cloned.1.call-done = bf16[1792,4096]{1,0:T(8,128)(2,1)} async-done(((bf16[1792,256]{1,0:T(8,128)(2,1)}), bf16[1792,4096]{1,0:T(8,128)(2,1)}) %all-gather.3.cloned.1.call-update) | async-done | bytes 14680080 | tf_op jit(solution)/shard_map/all_gather | solution.py:64
  124.1 10.3 %constant_dynamic-update-slice_fusion.2 = (bf16[32,6400]{1,0:T(8,128)(2,1)S(1)}, bf16[32,1792]{1,0:T(8,128)(2,1)}, f32[32,1792]{1,0:T(8,128)S(1)}) fusion(bf16[32,6400]{1,0:T(8,128)(2,1)S(1)} %constant_dynamic-update-slice_fusion.3, bf16[32,1792]{1,0:T(8,128)(2,1)} %param.16, bf16[32,1792]{1,0:T(8,128)(2,1)} %param.17, bf16[32,4096]{1,0:T(8,128)(2,1)} %param.18, ...), kind=kOutput, calls=%fused_computation.65 | convolution fusion | flops 470450176 | bytes 15630336 | tf_op jit(solution)/shard_map/dot_general | solution.py:49
  139.2 16.7 %multiply_convert_fusion = (bf16[256,1792]{1,0:T(8,128)(2,1)}, bf16[256,1792]{1,0:T(8,128)(2,1)}, bf16[256,1792]{1,0:T(8,128)(2,1)S(1)}) fusion(bf16[256,1792]{1,0:T(8,128)(2,1)} %param.12, bf16[256,1792]{1,0:T(8,128)(2,1)} %param.13, bf16[256,4096]{1,0:T(8,128)(2,1)S(1)} %copy-done, bf16[1792,4096]{1,0:T(8,128)(2,1)} %all-gather.3.cloned.1.call-done), kind=kOutput, calls=%fused_computation.27 | convolution fusion | flops 3765895168 | bytes 21364736 | tf_op jit(solution)/shard_map/dot_general | solution.py:49
  162.2 37.7 %all-gather.5.cloned.1.call-done = bf16[512,6400]{1,0:T(8,128)(2,1)} async-done(((bf16[32,6400]{1,0:T(8,128)(2,1)}), bf16[512,6400]{1,0:T(8,128)(2,1)}) %all-gather.5.cloned.1.call-update) | async-done | bytes 6553616 | tf_op jit(solution)/shard_map/all_gather | solution.py:13
  202.2 4.1 %split.17 = bf16[512,3584]{1,0:T(8,128)(2,1)} slice(bf16[512,6400]{1,0:T(8,128)(2,1)} %all-gather.5.cloned.1.call-done), slice={[0:512], [512:4096]} | slice | bytes 7340032 | tf_op jit(solution)/shard_map/split | solution.py:14
  206.3 2.9 split.18
  209.2 92.0 %while.15 = (s32[]{:T(128)}, f32[4,512,256]{2,1,0:T(8,128)}, s32[]{:T(128)}, bf16[512,512]{1,0:T(8,128)(2,1)}, bf16[256,512]{1,0:T(8,128)(2,1)S(1)}, /*index=5*/...) while((s32[]{:T(128)}, f32[4,512,256]{2,1,0:T(8,128)}, ...), condition=%wide.region_1.2_spmd, body=%wide.region_0.1_spmd.sunk | while | flops 104955920 | bytes 4079960 | solution.py:105
  211.4 2.3 convolution_bitcast_fusion.15
  217.6 2.3 convolution_bitcast_fusion.15
  223.7 2.3 convolution_bitcast_fusion.15
  229.9 2.3 convolution_bitcast_fusion.15
  236.0 2.3 convolution_bitcast_fusion.15
  242.1 2.3 convolution_bitcast_fusion.15
  254.4 2.3 convolution_bitcast_fusion.15
  260.5 2.3 convolution_bitcast_fusion.15
  272.8 2.3 convolution_bitcast_fusion.15
  278.9 2.3 convolution_bitcast_fusion.15
  285.0 2.3 convolution_bitcast_fusion.15
  297.3 2.3 convolution_bitcast_fusion.15
  301.2 2.9 copy.19
  304.1 3.2 copy.20
  307.3 4.5 %all-to-all-start = ((f32[8,4,512,32]{2,3,1,0:T(8,128)}), f32[8,4,512,32]{2,3,1,0:T(8,128)}, u32[]{:S(2)}, u32[]{:S(2)}) async-start(f32[8,4,512,32]{2,3,1,0:T(8,128)} %copy.20), calls=%async_computation | async-start | bytes 4194304 | tf_op jit(solution)/shard_map/all_to_all | solution.py:24
  311.8 26.6 %all-to-all-done = f32[8,4,512,32]{2,3,1,0:T(8,128)} async-done(((f32[8,4,512,32]{2,3,1,0:T(8,128)}), f32[8,4,512,32]{2,3,1,0:T(8,128)}, u32[]{:S(2)}, u32[]{:S(2)}) %all-to-all-start) | async-done | bytes 2097184 | tf_op jit(solution)/shard_map/all_to_all | solution.py:24
  340.7 9.6 %all_to_all.10 = f32[8,1,2]{2,1,0:T(1,128)S(1)} all-to-all(f32[8,1,2]{2,1,0:T(1,128)S(1)} %broadcast_in_dim.10), channel_id=1, replica_groups=mesh['dp'=16,'hid'=8] {'hid'}, dimensions={0} | all-to-all | bytes 128 | tf_op jit(solution)/shard_map/all_to_all | solution.py:30
  (111 shorter events, 82.2 us)
Async XLA Ops:
  7.2 129.6 %copy-start = (bf16[256,4096]{1,0:T(8,128)(2,1)S(1)}, bf16[256,4096]{1,0:T(8,128)(2,1)}, u32[]{:S(2)}) copy-start(bf16[256,4096]{1,0:T(8,128)(2,1)} %param.14) | copy-start | bytes 6291460
  7.2 116.9 %all-gather.3.cloned.1.call-start = ((), (), s32[]{:S(2)}) async-start(), calls=%async_computation.2 | async-start | bytes 15597568 | tf_op jit(solution)/shard_map/all_gather | solution.py:64
  7.9 192.1 %all-gather.5.cloned.1.call-start = ((), (), s32[]{:S(2)}) async-start(), calls=%async_computation.3 | async-start | bytes 6963200 | tf_op jit(solution)/shard_map/all_gather | solution.py:13
  8.7 125.7 %copy-start.2 = (bf16[32,1792]{1,0:T(8,128)(2,1)S(1)}, bf16[32,1792]{1,0:T(8,128)(2,1)}, u32[]{:S(2)}) copy-start(bf16[32,1792]{1,0:T(8,128)(2,1)} %param.16) | copy-start | bytes 344068
  8.7 126.4 %copy-start.7 = (bf16[32,1792]{1,0:T(8,128)(2,1)S(1)}, bf16[32,1792]{1,0:T(8,128)(2,1)}, u32[]{:S(2)}) copy-start(bf16[32,1792]{1,0:T(8,128)(2,1)} %param.17) | copy-start | bytes 344068
  134.4 4.0 %copy-start.1 = (bf16[256,512]{1,0:T(8,128)(2,1)S(1)}, bf16[256,512]{1,0:T(8,128)(2,1)}, u32[]{:S(2)}) copy-start(bf16[256,512]{1,0:T(8,128)(2,1)} %param.11) | copy-start | bytes 786436
  134.4 4.0 %copy-start.9 = (bf16[32,512]{1,0:T(8,128)(2,1)S(1)}, bf16[32,512]{1,0:T(8,128)(2,1)}, u32[]{:S(2)}) copy-start(bf16[32,512]{1,0:T(8,128)(2,1)} %param.15) | copy-start | bytes 98308
  136.0 0.8 copy-start.6
  155.9 2.3 copy-start.3
  155.9 2.3 copy-start.8
  158.2 2.0 copy-start.10
  158.2 2.0 copy-start.11
  158.2 2.7 copy-start.4
  158.2 2.6 copy-start.5
  307.3 31.1 %all-to-all-start = ((f32[8,4,512,32]{2,3,1,0:T(8,128)}), f32[8,4,512,32]{2,3,1,0:T(8,128)}, u32[]{:S(2)}, u32[]{:S(2)}) async-start(f32[8,4,512,32]{2,3,1,0:T(8,128)} %copy.20), calls=%async_computation | async-start | bytes 4194304 | tf_op jit(solution)/shard_map/all_to_all | solution.py:24
Sparse Core Ops, SparseCore 0:
  10.3 113.7 all-gather.2
  136.9 63.0 all-gather.4
where the time goes:
time: 361 us; the launch traced here: 358 us
  waiting for transfers between devices  180 us (50%)
  matrix products  114 us (32%)
  local copies, waits for them, and re-layouts  19.3 us (5%)
  other arithmetic  15.4 us (4%)
  between operations  14.2 us (4%)
  blocking collectives  9.56 us (3%)
  starting transfers between devices  4.53 us (1%)
    all_gather x1, waiting for transfers between devices, per_device(): piece = lax.all_gather(down_weight, 'dp', axis=1, tiled=True)  115 us
    dot_general x66, matrix products, pair_dot(): lax.dot_general(left, right, (((1,), (1,)), ((), ())), preferred_element_...  114 us
    all_gather x1, waiting for transfers between devices, side_by_side(): filled = lax.all_gather(both, axis, axis=dim, tiled=True)  37.7 us
    all_to_all x1, waiting for transfers between devices, sum_at_owner(): lax.all_to_all(parts, axis, split_axis=0, concat_axis=0, tiled=True)  26.6 us
    dynamic_update_slice x16, other arithmetic, absorb(): lax.dynamic_update_slice(state, grams(block), (0, source * val_rows, 0))  10.8 us
    all_to_all x1, blocking collectives, sent_to_all(): return lax.all_to_all(copies, axis, split_axis=0, concat_axis=0, tiled=True)  9.56 us
    split x3, local copies, waits for them, and re-layouts, side_by_side(): jnp.split(filled, [sum(widths[:k]) for k in range(1, len(widths))], axis=...  9.24 us
  transfers between devices with their start and end apart: 3, of which 3 were waited for; matrix products, arithmetic and copies ran while one was open for 7% of the time, Pallas kernels for 0%

commit v1 on v0

--- a/solution.py
+++ b/solution.py
@@ -61,7 +61,8 @@
     width = train_x.shape[1]
     n_seq = tok_rows // LEN
     n_val = val_rows * n_dp // LEN
-    piece = lax.all_gather(down_weight, "dp", axis=1, tiled=True)
+    stack = jnp.stack([down_weight] * lax.axis_size("dp"))
+    piece = jnp.concatenate(lax.all_to_all(stack, "dp", 0, 0), axis=1)
     cot_train = pair_dot(train_dy, piece)
     cot_val = pair_dot(val_dy, piece)
     hidden, gate_grad, up_grad = backward_parts(cot_train, gate_pre, up_pre)

time: 361 us -> 457 us (1.27)
  waiting for transfers between devices: 180 us -> 274 us
  matrix products: 114 us -> 102 us
  local copies, waits for them, and re-layouts: 19.3 us -> 26.6 us
  starting transfers between devices: 4.53 us -> 11.8 us
    all_to_all x0 -> x1, waiting for transfers between devices: none -> 197 us  [per_device(): piece = jnp.concatenate(lax.all_to_all(stack, 'dp', 0, 0), axis=1)]
    all_gather x1 -> x0, waiting for transfers between devices: 115 us -> none  [per_device(): piece = lax.all_gather(down_weight, 'dp', axis=1, tiled=True)]
    all_gather x1, waiting for transfers between devices: 37.7 us -> 50.9 us  [side_by_side(): filled = lax.all_gather(both, axis, axis=dim, tiled=True)]
    dot_general x66, matrix products: 114 us -> 102 us  [pair_dot(): lax.dot_general(left, right, (((1,), (1,)), ((), ())), preferred_element_...]
    all_to_all x0 -> x1, starting transfers between devices: none -> 7.33 us  [per_device(): piece = jnp.concatenate(lax.all_to_all(stack, 'dp', 0, 0), axis=1)]
    another operation x0 -> x1, local copies, waits for them, and re-layouts: none -> 6.58 us  [per_device(): stack = jnp.stack([down_weight] * lax.axis_size('dp'))]
  transfers between devices with their start and end apart: 3 -> 3, of which waited for: 3 -> 3; matrix products, arithmetic and copies ran while one was open for 7% -> 3% of each run, Pallas kernels for 0% -> 0%
where the time goes in v1:
time: 457 us; the launch traced here: 454 us
  waiting for transfers between devices  274 us (60%)
  matrix products  102 us (22%)
  local copies, waits for them, and re-layouts  26.6 us (6%)
  other arithmetic  15.4 us (3%)
  between operations  14.2 us (3%)
  starting transfers between devices  11.8 us (3%)
  blocking collectives  9.57 us (2%)
    all_to_all x1, waiting for transfers between devices, per_device(): piece = jnp.concatenate(lax.all_to_all(stack, 'dp', 0, 0), axis=1)  197 us
    dot_general x66, matrix products, pair_dot(): lax.dot_general(left, right, (((1,), (1,)), ((), ())), preferred_element_...  102 us
    all_gather x1, waiting for transfers between devices, side_by_side(): filled = lax.all_gather(both, axis, axis=dim, tiled=True)  50.9 us
    all_to_all x1, waiting for transfers between devices, sum_at_owner(): lax.all_to_all(parts, axis, split_axis=0, concat_axis=0, tiled=True)  26.6 us
    dynamic_update_slice x16, other arithmetic, absorb(): lax.dynamic_update_slice(state, grams(block), (0, source * val_rows, 0))  10.8 us
    all_to_all x1, blocking collectives, sent_to_all(): return lax.all_to_all(copies, axis, split_axis=0, concat_axis=0, tiled=True)  9.57 us
    split x3, local copies, waits for them, and re-layouts, side_by_side(): jnp.split(filled, [sum(widths[:k]) for k in range(1, len(widths))], axis=...  9.24 us
  transfers between devices with their start and end apart: 3, of which 3 were waited for; matrix products, arithmetic and copies ran while one was open for 3% of the time, Pallas kernels for 0%

profile of v1, /device:TPU:0, one launch (start us, length us, event | category | flops | bytes accessed | tf_op | source)
XLA Modules:
  0.0 454.0 jit_solution(4025451079586837540)
XLA Ops:
  8.8 6.6 %stack.84 = bf16[16,1792,256]{1,2,0:T(8,128)(2,1)} broadcast(bf16[1792,256]{0,1:T(8,128)(2,1)S(1)} %copy.22), dimensions={1,2} | broadcast | bytes 15597568 | tf_op jit(solution)/shard_map/stack | solution.py:64
  15.4 7.3 %all-to-all-start = ((bf16[16,1792,256]{1,2,0:T(8,128)(2,1)}), bf16[16,1792,256]{1,2,0:T(8,128)(2,1)}, u32[]{:S(2)}, u32[]{:S(2)}) async-start(bf16[16,1792,256]{1,2,0:T(8,128)(2,1)} %stack.84), calls=%async_computation | async-start | bytes 29360128 | tf_op jit(solution)/shard_map/all_to_all | solution.py:65
  22.8 196.7 %all-to-all-done = bf16[16,1792,256]{1,2,0:T(8,128)(2,1)} async-done(((bf16[16,1792,256]{1,2,0:T(8,128)(2,1)}), bf16[16,1792,256]{1,2,0:T(8,128)(2,1)}, u32[]{:S(2)}, u32[]{:S(2)}) %all-to-all-start) | async-done | bytes 14680096 | tf_op jit(solution)/shard_map/all_to_all | solution.py:65
  219.6 8.4 %constant_dynamic-update-slice_fusion.2 = (bf16[32,6400]{1,0:T(8,128)(2,1)S(1)}, bf16[32,1792]{1,0:T(8,128)(2,1)}, f32[32,1792]{1,0:T(8,128)S(1)}) fusion(bf16[32,6400]{1,0:T(8,128)(2,1)S(1)} %constant_dynamic-update-slice_fusion.3, bf16[32,1792]{1,0:T(8,128)(2,1)S(1)} %copy-done.2, bf16[32,1792]{1,0:T(8,128)(2,1)S(1)} %copy-done.8, ...), kind=kOutput, calls=%fused_computation.65 | convolution fusion | flops 470450176 | bytes 15630336 | tf_op jit(solution)/shard_map/dot_general | solution.py:49
  230.0 10.1 %multiply_convert_fusion = (bf16[256,1792]{1,0:T(8,128)(2,1)S(1)}, bf16[256,1792]{1,0:T(8,128)(2,1)S(1)}, bf16[256,1792]{1,0:T(8,128)(2,1)S(1)}) fusion(bf16[256,1792]{1,0:T(8,128)(2,1)} %param.12, bf16[256,1792]{1,0:T(8,128)(2,1)} %param.13, bf16[256,4096]{1,0:T(8,128)(2,1)S(1)} %copy-done, bf16[1792,4096]{0,1:T(8,128)(2,1)} %bitcast.5), kind=kOutput, calls=%fused_computation.27 | convolution fusion | flops 3765895168 | bytes 21364736 | tf_op jit(solution)/shard_map/dot_general | solution.py:49
  245.4 50.9 %all-gather.2.cloned.1.call-done = bf16[512,6400]{1,0:T(8,128)(2,1)} async-done(((bf16[32,6400]{1,0:T(8,128)(2,1)}), bf16[512,6400]{1,0:T(8,128)(2,1)}) %all-gather.2.cloned.1.call-update) | async-done | bytes 6553616 | tf_op jit(solution)/shard_map/all_gather | solution.py:13
  298.5 4.1 split.17
  302.5 2.9 split.18
  305.5 92.0 %while.15 = (s32[]{:T(128)}, f32[4,512,256]{2,1,0:T(8,128)}, s32[]{:T(128)}, bf16[512,512]{1,0:T(8,128)(2,1)}, bf16[256,512]{1,0:T(8,128)(2,1)S(1)}, /*index=5*/...) while((s32[]{:T(128)}, f32[4,512,256]{2,1,0:T(8,128)}, ...), condition=%wide.region_1.2_spmd, body=%wide.region_0.1_spmd.sunk | while | flops 104955920 | bytes 4079960 | solution.py:106
  307.7 2.3 convolution_bitcast_fusion.15
  320.0 2.3 convolution_bitcast_fusion.15
  326.1 2.3 convolution_bitcast_fusion.15
  332.2 2.3 convolution_bitcast_fusion.15
  338.4 2.3 convolution_bitcast_fusion.15
  344.5 2.3 convolution_bitcast_fusion.15
  350.6 2.3 convolution_bitcast_fusion.15
  356.8 2.3 convolution_bitcast_fusion.15
  362.9 2.3 convolution_bitcast_fusion.15
  393.6 2.3 convolution_bitcast_fusion.15
  397.5 2.9 copy.23
  400.4 3.2 copy.24
  403.6 4.5 all-to-all-start.1
  408.0 26.6 %all-to-all-done.1 = f32[8,4,512,32]{2,3,1,0:T(8,128)} async-done(((f32[8,4,512,32]{2,3,1,0:T(8,128)}), f32[8,4,512,32]{2,3,1,0:T(8,128)}, u32[]{:S(2)}, u32[]{:S(2)}) %all-to-all-start.1) | async-done | bytes 2097184 | tf_op jit(solution)/shard_map/all_to_all | solution.py:24
  437.0 9.6 %all_to_all.15 = f32[8,1,2]{2,1,0:T(1,128)S(1)} all-to-all(f32[8,1,2]{2,1,0:T(1,128)S(1)} %broadcast_in_dim.10), channel_id=1, replica_groups=mesh['dp'=16,'hid'=8] {'hid'}, dimensions={0} | all-to-all | bytes 128 | tf_op jit(solution)/shard_map/all_to_all | solution.py:30
  (114 shorter events, 83.1 us)
Async XLA Ops:
  7.2 222.4 %copy-start = (bf16[256,4096]{1,0:T(8,128)(2,1)S(1)}, bf16[256,4096]{1,0:T(8,128)(2,1)}, u32[]{:S(2)}) copy-start(bf16[256,4096]{1,0:T(8,128)(2,1)} %param.14) | copy-start | bytes 6291460
  15.4 7.4 %copy-start.10 = (bf16[32,512]{1,0:T(8,128)(2,1)S(1)}, bf16[32,512]{1,0:T(8,128)(2,1)}, u32[]{:S(2)}) copy-start(bf16[32,512]{1,0:T(8,128)(2,1)} %param.15) | copy-start | bytes 98308
  15.4 204.2 %copy-start.2 = (bf16[32,1792]{1,0:T(8,128)(2,1)S(1)}, bf16[32,1792]{1,0:T(8,128)(2,1)}, u32[]{:S(2)}) copy-start(bf16[32,1792]{1,0:T(8,128)(2,1)} %param.16) | copy-start | bytes 344068
  15.4 204.2 %copy-start.6 = (bf16[32,4096]{1,0:T(8,128)(2,1)S(1)}, bf16[32,4096]{1,0:T(8,128)(2,1)}, u32[]{:S(2)}) copy-start(bf16[32,4096]{1,0:T(8,128)(2,1)} %param.18) | copy-start | bytes 786436
  15.4 204.2 %copy-start.8 = (bf16[32,1792]{1,0:T(8,128)(2,1)S(1)}, bf16[32,1792]{1,0:T(8,128)(2,1)}, u32[]{:S(2)}) copy-start(bf16[32,1792]{1,0:T(8,128)(2,1)} %param.17) | copy-start | bytes 344068
  15.4 204.2 %all-to-all-start = ((bf16[16,1792,256]{1,2,0:T(8,128)(2,1)}), bf16[16,1792,256]{1,2,0:T(8,128)(2,1)}, u32[]{:S(2)}, u32[]{:S(2)}) async-start(bf16[16,1792,256]{1,2,0:T(8,128)(2,1)} %stack.84), calls=%async_computation | async-start | bytes 29360128 | tf_op jit(solution)/shard_map/all_to_all | solution.py:65
  22.7 273.5 %all-gather.2.cloned.1.call-start = ((), (), s32[]{:S(2)}) async-start(), calls=%async_computation.3 | async-start | bytes 6963200 | tf_op jit(solution)/shard_map/all_gather | solution.py:13
  228.0 1.9 copy-start.1
  228.8 0.8 copy-start.7
  230.0 10.2 %copy-start.11 = (bf16[32,1792]{1,0:T(8,128)(2,1)S(1)}, bf16[32,1792]{1,0:T(8,128)(2,1)}, u32[]{:S(2)}) copy-start(bf16[32,1792]{1,0:T(8,128)(2,1)} %get-tuple-element.292) | copy-start | bytes 344068
  230.0 10.2 %copy-start.12 = (bf16[32,1792]{1,0:T(8,128)(2,1)S(1)}, bf16[32,1792]{1,0:T(8,128)(2,1)}, u32[]{:S(2)}) copy-start(bf16[32,1792]{1,0:T(8,128)(2,1)} %get-tuple-element.294) | copy-start | bytes 344068
  240.1 3.9 copy-start.4
  240.1 3.9 copy-start.5
  240.2 1.0 copy-start.3
  240.2 1.2 copy-start.9
  403.6 31.1 %all-to-all-start.1 = ((f32[8,4,512,32]{2,3,1,0:T(8,128)}), f32[8,4,512,32]{2,3,1,0:T(8,128)}, u32[]{:S(2)}, u32[]{:S(2)}) async-start(f32[8,4,512,32]{2,3,1,0:T(8,128)} %copy.24), calls=%async_computation.1 | async-start | bytes 4194304 | tf_op jit(solution)/shard_map/all_to_all | solution.py:24
Sparse Core Ops, SparseCore 0:
  229.7 66.4 all-gather.1
